TPU v7x, 32 devices: a whole 2x2x4 slice. The times are simulated.
32 devices in a mesh: rows: 8 (over z, y), rep: 4 (over x, core).
Axes of the slice: x: 2, y: 2, z: 4, core: 2. Of those that a mesh axis runs over, the one named last changes fastest.
Arguments:
- embed: bfloat16 [4096, 1024], P('rows'), may hold values from -6 to 6
- start: bfloat16 [4096, 128], P('rows'), may hold values from -6 to 6
- links: int32 [8, 8], P('rows'), may hold values from -1 to 3, as said below
Outputs:
- embedding: float32 [4096, 128], P('rows')
Inputs may be any that keep to these rules, and one draw needn't show every extreme that they name: `links`: entry [r, s] is -1 (no pair) or a block of owner s; the diagonal is -1; each row has at most 6 entries other than -1, and some row has exactly 6.
All inputs are finite; a program needn't handle non-finite values.
Results may differ from a plain program's by a relative error of at most 0.012.
Values may be sent and summed in bfloat16 or wider, within the bound.
A program may use at most 128 MiB of HBM per device.

v0:
```python
import math
import jax
import jax.numpy as jnp
from jax import lax
from jax.sharding import PartitionSpec as P

BLOCK = 128
BLOCKS_DEV = 4
ITERS = 2
EPSILON = 1e-06


def row_scale(rows):
    values = rows.astype(jnp.float32)
    return lax.rsqrt(jnp.mean(values * values, axis=-1) + EPSILON)


def orthonormal(result, gram_matrix):
    lower_factor = jnp.linalg.cholesky(gram_matrix)
    return lax.linalg.triangular_solve(
        lower_factor, result, left_side=False, lower=True, transpose_a=True
    )


def quarter_of(values, blocks, rep_count, quarter_index):
    shaped = values.reshape(
        (blocks, rep_count, values.shape[0] // (blocks * rep_count)) + values.shape[1:]
    )
    return lax.dynamic_index_in_dim(shaped, quarter_index, 1, keepdims=False)


def widen(block_part, rep_count, quarter_index):
    choose = (jnp.arange(rep_count) == quarter_index).astype(jnp.float32)
    expanded = block_part[:, None] * choose.reshape((1, rep_count) + (1,) * (block_part.ndim - 1))
    return expanded.reshape((-1,) + block_part.shape[2:])


def on_device(embed, start, links):
    rows_count = lax.axis_size("rows")
    rep_count = lax.axis_size("rep")
    quarter_index = lax.axis_index("rep")
    slab_rows, feature_count = embed.shape
    comp_count = start.shape[1]
    blocks = BLOCKS_DEV
    piece_rows = BLOCK // rep_count
    spread = 2.0 / math.sqrt(feature_count)
    highest = lax.Precision.HIGHEST
    slab_scale = row_scale(embed)
    own_quarter = quarter_of(embed, blocks, rep_count, quarter_index)
    quarter_scale = row_scale(own_quarter)
    link_row = links.reshape(rows_count)
    alive_dense = (link_row >= 0).astype(jnp.float32)
    asked_for = lax.all_to_all(
        links.reshape(rows_count, 1), "rows", split_axis=0, concat_axis=0, tiled=True
    )[:, 0]
    picked = jnp.clip(asked_for, 0, blocks - 1)
    placer = (asked_for[:, None] == jnp.arange(blocks)[None, :]).astype(jnp.float32)
    outgoing = jnp.take(own_quarter, picked, axis=0)
    pieces = lax.all_to_all(outgoing, "rows", split_axis=0, concat_axis=0, tiled=True)
    piece_scale = row_scale(pieces)
    products_in = jnp.einsum("pnd,rd->pnr", pieces, embed, preferred_element_type=jnp.float32)
    exponent = spread * products_in * piece_scale[:, :, None] * slab_scale[None, None, :]
    pair_tiles = (jnp.exp(exponent) * alive_dense[:, None, None]).astype(jnp.bfloat16)
    diag_products = jnp.einsum(
        "bnd,rd->bnr", own_quarter, embed, preferred_element_type=jnp.float32
    )
    diag_exponent = spread * diag_products * quarter_scale[:, :, None] * slab_scale[None, None, :]
    row_ids = (
        jnp.arange(blocks)[:, None] * BLOCK
        + quarter_index * piece_rows
        + jnp.arange(piece_rows)[None, :]
    )
    self_mask = row_ids[:, :, None] == jnp.arange(slab_rows)[None, None, :]
    diag_tile = (
        jnp.where(self_mask, 0.0, jnp.exp(diag_exponent))
        .astype(jnp.bfloat16)
        .reshape(blocks * piece_rows, slab_rows)
    )
    own_sums = jnp.sum(pair_tiles, axis=(0, 1), dtype=jnp.float32) + jnp.sum(
        diag_tile, axis=0, dtype=jnp.float32
    )
    back_sums = jnp.sum(pair_tiles, axis=2, dtype=jnp.float32)
    got_sums = lax.all_to_all(back_sums, "rows", split_axis=0, concat_axis=0, tiled=True)
    placed_sums = jnp.dot(placer.T, got_sums, precision=highest)
    degree = lax.psum(own_sums + widen(placed_sums, rep_count, quarter_index), "rep")
    inv_root = lax.rsqrt(degree)
    current = start.astype(jnp.float32)
    scaled = (current * inv_root[:, None]).astype(jnp.bfloat16)
    for turn_index in range(ITERS):
        scaled_quarter = quarter_of(scaled, blocks, rep_count, quarter_index)
        outgoing_iterate = jnp.take(scaled_quarter, picked, axis=0)
        reverse = jnp.einsum("pnr,rk->pnk", pair_tiles, scaled, preferred_element_type=jnp.float32)
        returned = lax.all_to_all(reverse, "rows", split_axis=0, concat_axis=0, tiled=True)
        fetched = lax.all_to_all(outgoing_iterate, "rows", split_axis=0, concat_axis=0, tiled=True)
        forward = lax.dot_general(
            pair_tiles, fetched, (((0, 1), (0, 1)), ((), ())), preferred_element_type=jnp.float32
        )
        forward = forward + lax.dot_general(
            diag_tile,
            scaled_quarter.reshape(blocks * piece_rows, comp_count),
            (((0,), (0,)), ((), ())),
            preferred_element_type=jnp.float32,
        )
        placed = jnp.einsum("pb,pnk->bnk", placer, returned, precision=highest)
        summed_part = forward + widen(placed, rep_count, quarter_index)
        summed_all = lax.psum(summed_part, "rep")
        result = summed_all * inv_root[:, None]
        gram_matrix = lax.psum(jnp.dot(result.T, result, precision=highest), "rows")
        current = orthonormal(result, gram_matrix)
        scaled = (current * inv_root[:, None]).astype(jnp.bfloat16)
    return current * math.sqrt(slab_rows * rows_count)


def solution(mesh):
    return jax.shard_map(
        on_device,
        mesh=mesh,
        in_specs=(P("rows", None), P("rows", None), P("rows", None)),
        out_specs=P("rows", None),
        check_vma=False,
    )
```

profile of v0, /device:TPU:0, one launch (start us, length us, event | category | flops | bytes accessed | tf_op | source)
XLA Modules:
  0.0 369.6 jit_solution(8929522240494461467)
XLA Ops:
  6.5 1.4 copy.25
  7.9 7.3 %all-to-all-start = ((s32[8,1,1]{2,1,0:T(1,128)}), s32[8,1,1]{2,1,0:T(1,128)S(1)}, u32[]{:S(2)}, u32[]{:S(2)}) async-start(s32[8,1,1]{2,1,0:T(1,128)} %copy.25), calls=%async_computation | async-start | bytes 8192 | tf_op jit(solution)/shard_map/all_to_all | solution.py:53
  15.3 1.5 multiply_reduce_fusion
  17.2 4.5 %all-to-all-done = s32[8,1,1]{2,1,0:T(1,128)S(1)} async-done(((s32[8,1,1]{2,1,0:T(1,128)}), s32[8,1,1]{2,1,0:T(1,128)S(1)}, u32[]{:S(2)}, u32[]{:S(2)}) %all-to-all-start) | async-done | bytes 64 | tf_op jit(solution)/shard_map/all_to_all | solution.py:53
  23.6 3.5 all-to-all-start.1
  27.7 12.7 %all-to-all-done.1 = bf16[8,32,1024]{2,1,0:T(8,128)(2,1)S(1)} async-done(((bf16[8,32,1024]{2,1,0:T(8,128)(2,1)}), bf16[8,32,1024]{2,1,0:T(8,128)(2,1)S(1)}, u32[]{:S(2)}, u32[]{:S(2)}) %all-to-all-start.1) | async-done | bytes 524320 | tf_op jit(solution)/shard_map/all_to_all | solution.py:59
  40.6 1.2 convert_reduce_fusion.1
  41.8 3.7 all-to-all-start.2
  45.4 6.4 %all-to-all-done.2 = f32[8,1,32]{2,1,0:T(1,128)S(1)} async-done(((f32[8,1,32]{2,1,0:T(1,128)}), f32[8,1,32]{2,1,0:T(1,128)S(1)}, u32[]{:S(2)}, u32[]{:S(2)}) %all-to-all-start.2) | async-done | bytes 1056 | tf_op jit(solution)/shard_map/all_to_all | solution.py:83
  52.1 5.7 %psum.35 = f32[512]{0:T(512)S(1)} all-reduce(f32[512]{0:T(512)S(1)} %multiply_add_fusion), channel_id=1, replica_groups=mesh['rows'=8,'rep'=4] {'rep'}, use_global_device_ids=true, to_apply=%region_6.7 | all-reduce | flops 512 | bytes 4096 | tf_op jit(solution)/shard_map/psum | solution.py:85
  59.2 3.3 all-to-all-start.3
  63.4 6.0 %all-to-all-done.3 = bf16[8,32,128]{2,1,0:T(8,128)(2,1)S(1)} async-done(((bf16[8,32,128]{2,1,0:T(8,128)(2,1)}), bf16[8,32,128]{2,1,0:T(8,128)(2,1)S(1)}, u32[]{:S(2)}, u32[]{:S(2)}) %all-to-all-start.3) | async-done | bytes 65568 | tf_op jit(solution)/shard_map/all_to_all | solution.py:94
  69.4 3.4 all-to-all-start.4
  73.1 6.9 %all-to-all-done.4 = f32[8,32,128]{2,1,0:T(8,128)S(1)} async-done(((f32[8,32,128]{2,1,0:T(8,128)}), f32[8,32,128]{2,1,0:T(8,128)S(1)}, u32[]{:S(2)}, u32[]{:S(2)}) %all-to-all-start.4) | async-done | bytes 131104 | tf_op jit(solution)/shard_map/all_to_all | solution.py:93
  80.4 0.9 fusion.5
  81.4 30.4 %all-reduce.5.cloned.1.call-done = f32[512,128]{1,0:T(8,128)} async-done(((f32[512,128]{1,0:T(8,128)}), f32[512,128]{1,0:T(8,128)}) %all-reduce.5.cloned.1.call-update) | async-done | bytes 262160 | tf_op jit(solution)/shard_map/psum | solution.py:106
  111.8 2.5 fusion.19
  114.3 70.2 %all-reduce.7.cloned.1.call-done = f32[128,128]{0,1:T(8,128)} async-done(((f32[128,128]{0,1:T(8,128)}), f32[128,128]{0,1:T(8,128)}) %all-reduce.7.cloned.1.call-update) | async-done | bytes 65552 | tf_op jit(solution)/shard_map/psum | solution.py:108
  184.5 0.9 copy.30
  186.3 11.7 %cholesky.44 = f32[128,128]{1,0:T(8,128)S(1)} custom-call(f32[128,128]{1,0:T(8,128)S(1)} %fusion.38), custom_call_target="Cholesky" | custom-call | tf_op jit(solution)/shard_map/jit(cholesky)/cholesky | solution.py:19
  199.3 9.8 %custom-call.6 = f32[1,128,128]{1,2,0:T(8,128)S(1)} custom-call(f32[1,128,128]{2,1,0:T(8,128)S(1)} %fusion.33), custom_call_target="InvertDiagBlocksLowerTriangular" | custom-call | tf_op jit(solution)/shard_map/triangular_solve/custom-call.0 | solution.py:20
  210.9 4.5 %all-to-all-start.5 = ((bf16[8,32,128]{2,1,0:T(8,128)(2,1)}), bf16[8,32,128]{2,1,0:T(8,128)(2,1)S(1)}, u32[]{:S(2)}, u32[]{:S(2)}) async-start(bf16[8,32,128]{2,1,0:T(8,128)(2,1)} %broadcast_select_fusion.2), calls=%async_computation.5 | async-start | bytes 131072 | tf_op jit(solution)/shard_map/all_to_all | solution.py:94
  216.3 6.0 %all-to-all-done.5 = bf16[8,32,128]{2,1,0:T(8,128)(2,1)S(1)} async-done(((bf16[8,32,128]{2,1,0:T(8,128)(2,1)}), bf16[8,32,128]{2,1,0:T(8,128)(2,1)S(1)}, u32[]{:S(2)}, u32[]{:S(2)}) %all-to-all-start.5) | async-done | bytes 65568 | tf_op jit(solution)/shard_map/all_to_all | solution.py:94
  222.3 3.4 all-to-all-start.6
  226.2 6.8 %all-to-all-done.6 = f32[8,32,128]{2,1,0:T(8,128)S(1)} async-done(((f32[8,32,128]{2,1,0:T(8,128)}), f32[8,32,128]{2,1,0:T(8,128)S(1)}, u32[]{:S(2)}, u32[]{:S(2)}) %all-to-all-start.6) | async-done | bytes 131104 | tf_op jit(solution)/shard_map/all_to_all | solution.py:93
  233.4 0.9 fusion.4
  234.4 30.1 %all-reduce.9.cloned.1.call-done = f32[512,128]{1,0:T(8,128)} async-done(((f32[512,128]{1,0:T(8,128)}), f32[512,128]{1,0:T(8,128)}) %all-reduce.9.cloned.1.call-update) | async-done | bytes 262160 | tf_op jit(solution)/shard_map/psum | solution.py:106
  264.5 2.5 fusion.16
  267.0 70.0 %all-reduce.11.cloned.1.call-done = f32[128,128]{0,1:T(8,128)} async-done(((f32[128,128]{0,1:T(8,128)}), f32[128,128]{0,1:T(8,128)}) %all-reduce.11.cloned.1.call-update) | async-done | bytes 65552 | tf_op jit(solution)/shard_map/psum | solution.py:108
  337.0 0.9 copy.35
  338.8 11.7 %cholesky.55 = f32[128,128]{1,0:T(8,128)S(1)} custom-call(f32[128,128]{1,0:T(8,128)S(1)} %fusion.36), custom_call_target="Cholesky" | custom-call | tf_op jit(solution)/shard_map/jit(cholesky)/cholesky | solution.py:19
  351.9 9.8 %custom-call.7 = f32[1,128,128]{1,2,0:T(8,128)S(1)} custom-call(f32[1,128,128]{2,1,0:T(8,128)S(1)} %fusion.34), custom_call_target="InvertDiagBlocksLowerTriangular" | custom-call | tf_op jit(solution)/shard_map/triangular_solve/custom-call.0 | solution.py:20
  (72 shorter events, 15.5 us)
Async XLA Ops:
  6.5 10.3 %copy-start = (bf16[512,1024]{1,0:T(8,128)(2,1)S(1)}, bf16[512,1024]{1,0:T(8,128)(2,1)}, u32[]{:S(2)}) copy-start(bf16[512,1024]{1,0:T(8,128)(2,1)} %param.8) | copy-start | bytes 3145732
  7.9 13.7 %all-to-all-start = ((s32[8,1,1]{2,1,0:T(1,128)}), s32[8,1,1]{2,1,0:T(1,128)S(1)}, u32[]{:S(2)}, u32[]{:S(2)}) async-start(s32[8,1,1]{2,1,0:T(1,128)} %copy.25), calls=%async_computation | async-start | bytes 8192 | tf_op jit(solution)/shard_map/all_to_all | solution.py:53
  22.7 4.4 %copy-start.4 = (s32[1,8]{1,0:T(1,128)S(1)}, s32[1,8]{1,0:T(1,128)}, u32[]{:S(2)}) copy-start(s32[1,8]{1,0:T(1,128)} %param.10) | copy-start | bytes 100
  23.6 16.8 %all-to-all-start.1 = ((bf16[8,32,1024]{2,1,0:T(8,128)(2,1)}), bf16[8,32,1024]{2,1,0:T(8,128)(2,1)S(1)}, u32[]{:S(2)}, u32[]{:S(2)}) async-start(bf16[8,32,1024]{2,1,0:T(8,128)(2,1)} %broadcast_select_fusion), calls=%async_computation.1 | async-start | bytes 1048576 | tf_op jit(solution)/shard_map/all_to_all | solution.py:59
  40.5 17.2 %copy-start.3 = (bf16[512,128]{1,0:T(8,128)(2,1)S(1)}, bf16[512,128]{1,0:T(8,128)(2,1)}, u32[]{:S(2)}) copy-start(bf16[512,128]{1,0:T(8,128)(2,1)} %param.9) | copy-start | bytes 393220
  41.8 10.1 %all-to-all-start.2 = ((f32[8,1,32]{2,1,0:T(1,128)}), f32[8,1,32]{2,1,0:T(1,128)S(1)}, u32[]{:S(2)}, u32[]{:S(2)}) async-start(f32[8,1,32]{2,1,0:T(1,128)} %bitcast.6), calls=%async_computation.2 | async-start | bytes 8192 | tf_op jit(solution)/shard_map/all_to_all | solution.py:83
  59.2 10.2 %all-to-all-start.3 = ((bf16[8,32,128]{2,1,0:T(8,128)(2,1)}), bf16[8,32,128]{2,1,0:T(8,128)(2,1)S(1)}, u32[]{:S(2)}, u32[]{:S(2)}) async-start(bf16[8,32,128]{2,1,0:T(8,128)(2,1)} %broadcast_select_fusion.1), calls=%async_computation.3 | async-start | bytes 131072 | tf_op jit(solution)/shard_map/all_to_all | solution.py:94
  69.4 10.7 %all-to-all-start.4 = ((f32[8,32,128]{2,1,0:T(8,128)}), f32[8,32,128]{2,1,0:T(8,128)S(1)}, u32[]{:S(2)}, u32[]{:S(2)}) async-start(f32[8,32,128]{2,1,0:T(8,128)} %fusion.23), calls=%async_computation.4 | async-start | bytes 262144 | tf_op jit(solution)/shard_map/all_to_all | solution.py:93
  72.7 39.1 %all-reduce.5.cloned.1.call-start = ((), (), s32[]{:S(2)}) async-start(), calls=%async_computation.7 | async-start | bytes 524288 | tf_op jit(solution)/shard_map/psum | solution.py:106
  81.4 103.1 %all-reduce.7.cloned.1.call-start = ((), (), s32[]{:S(2)}) async-start(), calls=%async_computation.8 | async-start | bytes 131072 | tf_op jit(solution)/shard_map/psum | solution.py:108
  111.8 97.3 %copy-start.1 = (f32[512,128]{1,0:T(8,128)S(1)}, f32[512,128]{1,0:T(8,128)}, u32[]{:S(2)}) copy-start(f32[512,128]{1,0:T(8,128)} %all-reduce.5.cloned.1.call-done) | copy-start | bytes 786436
  210.9 11.4 %all-to-all-start.5 = ((bf16[8,32,128]{2,1,0:T(8,128)(2,1)}), bf16[8,32,128]{2,1,0:T(8,128)(2,1)S(1)}, u32[]{:S(2)}, u32[]{:S(2)}) async-start(bf16[8,32,128]{2,1,0:T(8,128)(2,1)} %broadcast_select_fusion.2), calls=%async_computation.5 | async-start | bytes 131072 | tf_op jit(solution)/shard_map/all_to_all | solution.py:94
  222.3 10.7 %all-to-all-start.6 = ((f32[8,32,128]{2,1,0:T(8,128)}), f32[8,32,128]{2,1,0:T(8,128)S(1)}, u32[]{:S(2)}, u32[]{:S(2)}) async-start(f32[8,32,128]{2,1,0:T(8,128)} %fusion.21), calls=%async_computation.6 | async-start | bytes 262144 | tf_op jit(solution)/shard_map/all_to_all | solution.py:93
  225.7 38.8 %all-reduce.9.cloned.1.call-start = ((), (), s32[]{:S(2)}) async-start(), calls=%async_computation.9 | async-start | bytes 524288 | tf_op jit(solution)/shard_map/psum | solution.py:106
  234.3 102.7 %all-reduce.11.cloned.1.call-start = ((), (), s32[]{:S(2)}) async-start(), calls=%async_computation.10 | async-start | bytes 131072 | tf_op jit(solution)/shard_map/psum | solution.py:108
  264.5 97.2 %copy-start.2 = (f32[512,128]{1,0:T(8,128)S(1)}, f32[512,128]{1,0:T(8,128)}, u32[]{:S(2)}) copy-start(f32[512,128]{1,0:T(8,128)} %all-reduce.9.cloned.1.call-done) | copy-start | bytes 786436
Sparse Core Ops, SparseCore 0:
  81.5 30.2 all-reduce.4
  115.2 69.2 all-reduce.6
  234.5 29.9 all-reduce.8
  267.8 69.2 all-reduce.10
where the time goes:
time: 371 us; the launch traced here: 370 us
  waiting for transfers between devices  250 us (67%)
  other arithmetic  52.4 us (14%)
  starting transfers between devices  29.4 us (8%)
  between operations  13.5 us (4%)
  matrix products  12.4 us (3%)
  local copies, waits for them, and re-layouts  6.14 us (2%)
  blocking collectives  5.65 us (2%)
    psum x2, waiting for transfers between devices, on_device(): gram_matrix = lax.psum(jnp.dot(result.T, result, precision=highest), 'rows')  140 us
    psum x2, waiting for transfers between devices, on_device(): summed_all = lax.psum(summed_part, 'rep')  60.5 us
    another operation x6, other arithmetic, orthonormal(): lower_factor = jnp.linalg.cholesky(gram_matrix)  24.8 us
    another operation x4, other arithmetic, orthonormal(): lax.linalg.triangular_solve(lower_factor, result, left_side=False, lower=...  20.9 us
    all_to_all x2, waiting for transfers between devices, on_device(): lax.all_to_all(reverse, 'rows', split_axis=0, concat_axis=0, tiled=True)  13.7 us
    all_to_all x1, waiting for transfers between devices, on_device(): lax.all_to_all(outgoing, 'rows', split_axis=0, concat_axis=0, tiled=True)  12.7 us
    all_to_all x2, waiting for transfers between devices, on_device(): lax.all_to_all(outgoing_iterate, 'rows', split_axis=0, concat_axis=0, til...  12 us
    all_to_all x2, starting transfers between devices, on_device(): lax.all_to_all(outgoing_iterate, 'rows', split_axis=0, concat_axis=0, til...  7.89 us
  transfers between devices with their start and end apart: 11, of which 11 were waited for; matrix products, arithmetic and copies ran while one was open for 1% of the time, Pallas kernels for 0%

commit v1 on v0

--- a/solution.py
+++ b/solution.py
@@ -105,7 +105,8 @@
         summed_part = forward + widen(placed, rep_count, quarter_index)
         summed_all = lax.psum(summed_part, "rep")
         result = summed_all * inv_root[:, None]
-        gram_matrix = lax.psum(jnp.dot(result.T, result, precision=highest), "rows")
+        advance_roads_up = lambda arr_in, a_name: jnp.sum(lax.all_gather(arr_in, a_name), 0)
+        gram_matrix = advance_roads_up(jnp.dot(result.T, result, precision=highest), "rows")
         current = orthonormal(result, gram_matrix)
         scaled = (current * inv_root[:, None]).astype(jnp.bfloat16)
     return current * math.sqrt(slab_rows * rows_count)

time: 371 us -> 289 us (0.78)
  waiting for transfers between devices: 250 us -> 109 us
  blocking collectives: 5.65 us -> 68.9 us
    psum x2 -> x0, waiting for transfers between devices: 140 us -> none  [on_device(): gram_matrix = lax.psum(jnp.dot(result.T, result, precision=highest), 'rows')]
    all_gather x0 -> x2, blocking collectives: none -> 63.2 us  [on_device(): lax.all_gather(arr_in, a_name)]
  transfers between devices with their start and end apart: 11 -> 9, of which waited for: 11 -> 9; matrix products, arithmetic and copies ran while one was open for 1% -> 2% of each run, Pallas kernels for 0% -> 0%
where the time goes in v1:
time: 289 us; the launch traced here: 288 us
  waiting for transfers between devices  109 us (38%)
  blocking collectives  68.9 us (24%)
  other arithmetic  50.8 us (18%)
  starting transfers between devices  30.1 us (10%)
  between operations  13.8 us (5%)
  matrix products  11.1 us (4%)
  local copies, waits for them, and re-layouts  4.47 us (2%)
    all_gather x2, blocking collectives, on_device(): lax.all_gather(arr_in, a_name)  63.2 us
    psum x2, waiting for transfers between devices, on_device(): summed_all = lax.psum(summed_part, 'rep')  59.7 us
    another operation x6, other arithmetic, orthonormal(): lower_factor = jnp.linalg.cholesky(gram_matrix)  24.8 us
    another operation x4, other arithmetic, orthonormal(): lax.linalg.triangular_solve(lower_factor, result, left_side=False, lower=...  20.9 us
    all_to_all x2, waiting for transfers between devices, on_device(): lax.all_to_all(reverse, 'rows', split_axis=0, concat_axis=0, tiled=True)  13.7 us
    all_to_all x1, waiting for transfers between devices, on_device(): lax.all_to_all(outgoing, 'rows', split_axis=0, concat_axis=0, tiled=True)  12.7 us
    all_to_all x2, waiting for transfers between devices, on_device(): lax.all_to_all(outgoing_iterate, 'rows', split_axis=0, concat_axis=0, til...  12 us
    all_to_all x2, starting transfers between devices, on_device(): lax.all_to_all(outgoing_iterate, 'rows', split_axis=0, concat_axis=0, til...  8.64 us
  transfers between devices with their start and end apart: 9, of which 9 were waited for; matrix products, arithmetic and copies ran while one was open for 2% of the time, Pallas kernels for 0%

profile of v1, /device:TPU:0, one launch (start us, length us, event | category | flops | bytes accessed | tf_op | source)
XLA Modules:
  0.0 288.2 jit_solution(2613524726807674382)
XLA Ops:
  6.5 1.4 copy.21
  7.9 7.3 %all-to-all-start = ((s32[8,1,1]{2,1,0:T(1,128)}), s32[8,1,1]{2,1,0:T(1,128)S(1)}, u32[]{:S(2)}, u32[]{:S(2)}) async-start(s32[8,1,1]{2,1,0:T(1,128)} %copy.21), calls=%async_computation | async-start | bytes 8192 | tf_op jit(solution)/shard_map/all_to_all | solution.py:53
  15.3 1.5 multiply_reduce_fusion
  17.2 4.5 %all-to-all-done = s32[8,1,1]{2,1,0:T(1,128)S(1)} async-done(((s32[8,1,1]{2,1,0:T(1,128)}), s32[8,1,1]{2,1,0:T(1,128)S(1)}, u32[]{:S(2)}, u32[]{:S(2)}) %all-to-all-start) | async-done | bytes 64 | tf_op jit(solution)/shard_map/all_to_all | solution.py:53
  22.7 0.9 broadcast_select_fusion
  23.6 3.5 %all-to-all-start.1 = ((bf16[8,32,1024]{2,1,0:T(8,128)(2,1)}), bf16[8,32,1024]{2,1,0:T(8,128)(2,1)S(1)}, u32[]{:S(2)}, u32[]{:S(2)}) async-start(bf16[8,32,1024]{2,1,0:T(8,128)(2,1)} %broadcast_select_fusion), calls=%async_computation.1 | async-start | bytes 1048576 | tf_op jit(solution)/shard_map/all_to_all | solution.py:59
  27.7 12.7 %all-to-all-done.1 = bf16[8,32,1024]{2,1,0:T(8,128)(2,1)S(1)} async-done(((bf16[8,32,1024]{2,1,0:T(8,128)(2,1)}), bf16[8,32,1024]{2,1,0:T(8,128)(2,1)S(1)}, u32[]{:S(2)}, u32[]{:S(2)}) %all-to-all-start.1) | async-done | bytes 524320 | tf_op jit(solution)/shard_map/all_to_all | solution.py:59
  40.6 1.2 convert_reduce_fusion.1
  41.8 3.7 %all-to-all-start.2 = ((f32[8,1,32]{2,1,0:T(1,128)}), f32[8,1,32]{2,1,0:T(1,128)S(1)}, u32[]{:S(2)}, u32[]{:S(2)}) async-start(f32[8,1,32]{2,1,0:T(1,128)} %bitcast.6), calls=%async_computation.2 | async-start | bytes 8192 | tf_op jit(solution)/shard_map/all_to_all | solution.py:83
  45.4 6.4 %all-to-all-done.2 = f32[8,1,32]{2,1,0:T(1,128)S(1)} async-done(((f32[8,1,32]{2,1,0:T(1,128)}), f32[8,1,32]{2,1,0:T(1,128)S(1)}, u32[]{:S(2)}, u32[]{:S(2)}) %all-to-all-start.2) | async-done | bytes 1056 | tf_op jit(solution)/shard_map/all_to_all | solution.py:83
  52.1 5.7 %psum.21 = f32[512]{0:T(512)S(1)} all-reduce(f32[512]{0:T(512)S(1)} %multiply_add_fusion), channel_id=1, replica_groups=mesh['rows'=8,'rep'=4] {'rep'}, use_global_device_ids=true, to_apply=%region_6.7 | all-reduce | flops 512 | bytes 4096 | tf_op jit(solution)/shard_map/psum | solution.py:85
  59.2 3.3 %all-to-all-start.3 = ((bf16[8,32,128]{2,1,0:T(8,128)(2,1)}), bf16[8,32,128]{2,1,0:T(8,128)(2,1)S(1)}, u32[]{:S(2)}, u32[]{:S(2)}) async-start(bf16[8,32,128]{2,1,0:T(8,128)(2,1)} %broadcast_select_fusion.1), calls=%async_computation.3 | async-start | bytes 131072 | tf_op jit(solution)/shard_map/all_to_all | solution.py:94
  62.5 0.9 fusion.23
  63.4 6.0 %all-to-all-done.3 = bf16[8,32,128]{2,1,0:T(8,128)(2,1)S(1)} async-done(((bf16[8,32,128]{2,1,0:T(8,128)(2,1)}), bf16[8,32,128]{2,1,0:T(8,128)(2,1)S(1)}, u32[]{:S(2)}, u32[]{:S(2)}) %all-to-all-start.3) | async-done | bytes 65568 | tf_op jit(solution)/shard_map/all_to_all | solution.py:94
  69.4 3.4 %all-to-all-start.4 = ((f32[8,32,128]{2,1,0:T(8,128)}), f32[8,32,128]{2,1,0:T(8,128)S(1)}, u32[]{:S(2)}, u32[]{:S(2)}) async-start(f32[8,32,128]{2,1,0:T(8,128)} %fusion.23), calls=%async_computation.4 | async-start | bytes 262144 | tf_op jit(solution)/shard_map/all_to_all | solution.py:93
  73.1 6.9 %all-to-all-done.4 = f32[8,32,128]{2,1,0:T(8,128)S(1)} async-done(((f32[8,32,128]{2,1,0:T(8,128)}), f32[8,32,128]{2,1,0:T(8,128)S(1)}, u32[]{:S(2)}, u32[]{:S(2)}) %all-to-all-start.4) | async-done | bytes 131104 | tf_op jit(solution)/shard_map/all_to_all | solution.py:93
  80.4 0.9 fusion.5
  81.4 30.4 %all-reduce.3.cloned.1.call-done = f32[512,128]{1,0:T(8,128)} async-done(((f32[512,128]{1,0:T(8,128)}), f32[512,128]{1,0:T(8,128)}) %all-reduce.3.cloned.1.call-update) | async-done | bytes 262160 | tf_op jit(solution)/shard_map/psum | solution.py:106
  111.8 1.9 fusion.19
  113.7 31.6 %all-gather = f32[1024,128]{1,0:T(8,128)S(1)} all-gather(f32[128,128]{1,0:T(8,128)S(1)} %fusion.19), channel_id=2, replica_groups=mesh['rows'=8,'rep'=4] {'rows'}, dimensions={0}, use_global_device_ids=true | all-gather | bytes 589824 | tf_op jit(solution)/shard_map/all_gather | solution.py:108
  145.4 11.7 %cholesky.44 = f32[128,128]{1,0:T(8,128)S(1)} custom-call(f32[128,128]{1,0:T(8,128)S(1)} %fusion.38), custom_call_target="Cholesky" | custom-call | tf_op jit(solution)/shard_map/jit(cholesky)/cholesky | solution.py:19
  158.5 9.8 %custom-call.6 = f32[1,128,128]{1,2,0:T(8,128)S(1)} custom-call(f32[1,128,128]{2,1,0:T(8,128)S(1)} %fusion.33), custom_call_target="InvertDiagBlocksLowerTriangular" | custom-call | tf_op jit(solution)/shard_map/triangular_solve/custom-call.0 | solution.py:20
  170.0 5.3 %all-to-all-start.5 = ((bf16[8,32,128]{2,1,0:T(8,128)(2,1)}), bf16[8,32,128]{2,1,0:T(8,128)(2,1)S(1)}, u32[]{:S(2)}, u32[]{:S(2)}) async-start(bf16[8,32,128]{2,1,0:T(8,128)(2,1)} %broadcast_select_fusion.2), calls=%async_computation.5 | async-start | bytes 131072 | tf_op jit(solution)/shard_map/all_to_all | solution.py:94
  176.2 6.0 %all-to-all-done.5 = bf16[8,32,128]{2,1,0:T(8,128)(2,1)S(1)} async-done(((bf16[8,32,128]{2,1,0:T(8,128)(2,1)}), bf16[8,32,128]{2,1,0:T(8,128)(2,1)S(1)}, u32[]{:S(2)}, u32[]{:S(2)}) %all-to-all-start.5) | async-done | bytes 65568 | tf_op jit(solution)/shard_map/all_to_all | solution.py:94
  182.2 3.4 %all-to-all-start.6 = ((f32[8,32,128]{2,1,0:T(8,128)}), f32[8,32,128]{2,1,0:T(8,128)S(1)}, u32[]{:S(2)}, u32[]{:S(2)}) async-start(f32[8,32,128]{2,1,0:T(8,128)} %fusion.21), calls=%async_computation.6 | async-start | bytes 262144 | tf_op jit(solution)/shard_map/all_to_all | solution.py:93
  186.1 6.8 %all-to-all-done.6 = f32[8,32,128]{2,1,0:T(8,128)S(1)} async-done(((f32[8,32,128]{2,1,0:T(8,128)}), f32[8,32,128]{2,1,0:T(8,128)S(1)}, u32[]{:S(2)}, u32[]{:S(2)}) %all-to-all-start.6) | async-done | bytes 131104 | tf_op jit(solution)/shard_map/all_to_all | solution.py:93
  193.3 0.9 fusion.4
  194.2 29.3 %all-reduce.5.cloned.1.call-done = f32[512,128]{1,0:T(8,128)} async-done(((f32[512,128]{1,0:T(8,128)}), f32[512,128]{1,0:T(8,128)}) %all-reduce.5.cloned.1.call-update) | async-done | bytes 262160 | tf_op jit(solution)/shard_map/psum | solution.py:106
  223.5 1.9 fusion.16
  225.3 31.6 %all-gather.1 = f32[1024,128]{1,0:T(8,128)S(1)} all-gather(f32[128,128]{1,0:T(8,128)S(1)} %fusion.16), channel_id=3, replica_groups=mesh['rows'=8,'rep'=4] {'rows'}, dimensions={0}, use_global_device_ids=true | all-gather | bytes 589824 | tf_op jit(solution)/shard_map/all_gather | solution.py:108
  257.1 11.7 %cholesky.55 = f32[128,128]{1,0:T(8,128)S(1)} custom-call(f32[128,128]{1,0:T(8,128)S(1)} %fusion.36), custom_call_target="Cholesky" | custom-call | tf_op jit(solution)/shard_map/jit(cholesky)/cholesky | solution.py:19
  270.2 9.8 %custom-call.7 = f32[1,128,128]{1,2,0:T(8,128)S(1)} custom-call(f32[1,128,128]{2,1,0:T(8,128)S(1)} %fusion.34), custom_call_target="InvertDiagBlocksLowerTriangular" | custom-call | tf_op jit(solution)/shard_map/triangular_solve/custom-call.0 | solution.py:20
  (70 shorter events, 12.2 us)
Async XLA Ops:
  6.5 10.3 %copy-start = (bf16[512,1024]{1,0:T(8,128)(2,1)S(1)}, bf16[512,1024]{1,0:T(8,128)(2,1)}, u32[]{:S(2)}) copy-start(bf16[512,1024]{1,0:T(8,128)(2,1)} %param.8) | copy-start | bytes 3145732
  7.9 13.7 %all-to-all-start = ((s32[8,1,1]{2,1,0:T(1,128)}), s32[8,1,1]{2,1,0:T(1,128)S(1)}, u32[]{:S(2)}, u32[]{:S(2)}) async-start(s32[8,1,1]{2,1,0:T(1,128)} %copy.21), calls=%async_computation | async-start | bytes 8192 | tf_op jit(solution)/shard_map/all_to_all | solution.py:53
  22.7 4.4 %copy-start.4 = (s32[1,8]{1,0:T(1,128)S(1)}, s32[1,8]{1,0:T(1,128)}, u32[]{:S(2)}) copy-start(s32[1,8]{1,0:T(1,128)} %param.10) | copy-start | bytes 100
  23.6 16.8 %all-to-all-start.1 = ((bf16[8,32,1024]{2,1,0:T(8,128)(2,1)}), bf16[8,32,1024]{2,1,0:T(8,128)(2,1)S(1)}, u32[]{:S(2)}, u32[]{:S(2)}) async-start(bf16[8,32,1024]{2,1,0:T(8,128)(2,1)} %broadcast_select_fusion), calls=%async_computation.1 | async-start | bytes 1048576 | tf_op jit(solution)/shard_map/all_to_all | solution.py:59
  40.5 17.2 %copy-start.3 = (bf16[512,128]{1,0:T(8,128)(2,1)S(1)}, bf16[512,128]{1,0:T(8,128)(2,1)}, u32[]{:S(2)}) copy-start(bf16[512,128]{1,0:T(8,128)(2,1)} %param.9) | copy-start | bytes 393220
  41.8 10.1 %all-to-all-start.2 = ((f32[8,1,32]{2,1,0:T(1,128)}), f32[8,1,32]{2,1,0:T(1,128)S(1)}, u32[]{:S(2)}, u32[]{:S(2)}) async-start(f32[8,1,32]{2,1,0:T(1,128)} %bitcast.6), calls=%async_computation.2 | async-start | bytes 8192 | tf_op jit(solution)/shard_map/all_to_all | solution.py:83
  59.2 10.2 %all-to-all-start.3 = ((bf16[8,32,128]{2,1,0:T(8,128)(2,1)}), bf16[8,32,128]{2,1,0:T(8,128)(2,1)S(1)}, u32[]{:S(2)}, u32[]{:S(2)}) async-start(bf16[8,32,128]{2,1,0:T(8,128)(2,1)} %broadcast_select_fusion.1), calls=%async_computation.3 | async-start | bytes 131072 | tf_op jit(solution)/shard_map/all_to_all | solution.py:94
  69.4 10.7 %all-to-all-start.4 = ((f32[8,32,128]{2,1,0:T(8,128)}), f32[8,32,128]{2,1,0:T(8,128)S(1)}, u32[]{:S(2)}, u32[]{:S(2)}) async-start(f32[8,32,128]{2,1,0:T(8,128)} %fusion.23), calls=%async_computation.4 | async-start | bytes 262144 | tf_op jit(solution)/shard_map/all_to_all | solution.py:93
  72.7 39.1 %all-reduce.3.cloned.1.call-start = ((), (), s32[]{:S(2)}) async-start(), calls=%async_computation.7 | async-start | bytes 524288 | tf_op jit(solution)/shard_map/psum | solution.py:106
  111.8 56.5 %copy-start.1 = (f32[512,128]{1,0:T(8,128)S(1)}, f32[512,128]{1,0:T(8,128)}, u32[]{:S(2)}) copy-start(f32[512,128]{1,0:T(8,128)} %all-reduce.3.cloned.1.call-done) | copy-start | bytes 786436
  170.0 12.2 %all-to-all-start.5 = ((bf16[8,32,128]{2,1,0:T(8,128)(2,1)}), bf16[8,32,128]{2,1,0:T(8,128)(2,1)S(1)}, u32[]{:S(2)}, u32[]{:S(2)}) async-start(bf16[8,32,128]{2,1,0:T(8,128)(2,1)} %broadcast_select_fusion.2), calls=%async_computation.5 | async-start | bytes 131072 | tf_op jit(solution)/shard_map/all_to_all | solution.py:94
  182.2 10.7 %all-to-all-start.6 = ((f32[8,32,128]{2,1,0:T(8,128)}), f32[8,32,128]{2,1,0:T(8,128)S(1)}, u32[]{:S(2)}, u32[]{:S(2)}) async-start(f32[8,32,128]{2,1,0:T(8,128)} %fusion.21), calls=%async_computation.6 | async-start | bytes 262144 | tf_op jit(solution)/shard_map/all_to_all | solution.py:93
  185.6 37.9 %all-reduce.5.cloned.1.call-start = ((), (), s32[]{:S(2)}) async-start(), calls=%async_computation.8 | async-start | bytes 524288 | tf_op jit(solution)/shard_map/psum | solution.py:106
  223.5 56.5 %copy-start.2 = (f32[512,128]{1,0:T(8,128)S(1)}, f32[512,128]{1,0:T(8,128)}, u32[]{:S(2)}) copy-start(f32[512,128]{1,0:T(8,128)} %all-reduce.5.cloned.1.call-done) | copy-start | bytes 786436
Sparse Core Ops, SparseCore 0:
  81.5 30.2 all-reduce.2
  194.3 29.1 all-reduce.4
